TPU v7x, 128 devices: a whole 4x4x4 slice. The times are simulated.
128 devices in a mesh: fluid: 32 (over x, z, core), solid: 4 (over y).
Axes of the slice: x: 4, y: 4, z: 4, core: 2. Of those that a mesh axis runs over, the one named last changes fastest.
Arguments:
- flow: bfloat16 [3, 1048576, 128], P(None, ('fluid', 'solid')), may hold values from -6 to 6
- wall_motion: float32 [3, 1048576], P(None, ('fluid', 'solid')), may hold values from -6 to 6
- normal_operator: bfloat16 [128, 128], replicated, may hold values from -0.5 to 0.5
- wall_coupling: float32 [128], replicated, may hold values from -4 to 4
- wall_stencil: bfloat16 [128], replicated, may hold values from -0.5 to 0.5
- rbf_blocks: bfloat16 [8192, 128, 128], P(('fluid', 'solid')), may hold values from -0.5 to 0.5
- block_owner: int32 [8192, 1], P(('fluid', 'solid')), may hold values from 0 to 31; in each aligned block of 64 rows (0 to 63, 64 to 127, ...) at most 3 rows name the same one
- block_row: int32 [8192, 1], P(('fluid', 'solid')), may hold values from 0 to 31
- displacement: float32 [4096, 3, 128], P(('fluid', 'solid')), may hold values from -6 to 6
- stiffness: float32 [4096, 128], P(('fluid', 'solid')), may hold values from 0.5 to 4
- residual_history: float32 [64, 4096, 3, 128], P(None, ('fluid', 'solid')), may hold values from -0.03827328 to 0.03827328
- solution_history: float32 [64, 4096, 3, 128], P(None, ('fluid', 'solid')), may hold values from -6 to 6
Outputs:
- new_flow: bfloat16 [3, 1048576, 128], P(None, ('fluid', 'solid'))
- next_displacement: float32 [4096, 3, 128], P(('fluid', 'solid'))
- wall_next: float32 [3, 1048576], P(None, ('fluid', 'solid'))
- residual_norm: float32 [], replicated
Inputs may be any that keep to these rules, and one draw needn't show every extreme that they name: `block_owner`: each device's 64 blocks name no owner more than 3 times, a bound that some block reaches; every owner gets some block.
All inputs are finite; a program needn't handle non-finite values.
Results may differ from a plain program's by a relative error of at most 0.0035.
The roundings to bfloat16 on the way count: a program that leaves them out, or rounds other values in their place, can miss the bound.
Values may be sent and summed in bfloat16 or wider, within the bound.
A program may use at most 128 MiB of HBM per device.

v0:
```python
import jax
import jax.numpy as jnp
from jax import lax
from jax.experimental import pallas as pl
from jax.experimental.pallas import tpu as pltpu
from jax.sharding import PartitionSpec as P

MESH = pl.DeviceIdType.MESH
F32 = jnp.float32
BF16 = jnp.bfloat16
SWEEPS = 4
NF = 32
NS = 4
ND = NF * NS
BLOCKS = 64
BLK = 128
POINTS = BLOCKS * BLK
EDGE = 16
CHUNKS = 8
ROWS = 32
HIST = 64
ENT = 96
SLOTS = 16


def iota(shape, dim):
    return lax.broadcasted_iota(jnp.int32, shape, dim)


def dot(a, b):
    return jnp.dot(a, b, preferred_element_type=F32)


def dot_t(a, b):
    return lax.dot_general(a, b, (((1,), (1,)), ((), ())), preferred_element_type=F32)


def halves(x):
    hi = x.astype(BF16)
    return hi, (x - hi.astype(F32)).astype(BF16)


def kernel(
    flow, wm, aop, wc, ws, rbf, owner, row, disp, stiff, vh, wh,
    nf, nd, local, norm, rbv,
    fbuf, wmv, av, wcv, wsv, ownv, rowv, dbuf, sbuf, vv, wv,
    mapped, oh, oht, lab, gsend, gin1, gsum1, gin2, out, arrived, pt, fext,
    psend, pin1, psum1, pin2, cbuf, rep, back, resid, wide32, tract,
    lsem, ssem, rsem,
):
    f, s = lax.axis_index("fluid"), lax.axis_index("solid")
    me = f * NS + s
    nxt, prv = lax.rem(me + 1, ND), lax.rem(me + ND - 1, ND)
    nxt_id, prv_id = (nxt // NS, lax.rem(nxt, NS)), (prv // NS, lax.rem(prv, NS))
    core, chip = lax.rem(f, 2), f // 2
    near = core * NS + s

    def near_id(d):
        other = lax.rem(near + d, 8)
        return other, (chip * 2 + other // NS, lax.rem(other, NS))

    def far_id(d):
        other = lax.rem(chip + d, 16)
        return other, (other * 2 + core, s)

    barrier = pltpu.get_barrier_semaphore()

    def signal(device):
        pl.semaphore_signal(barrier, inc=1, device_id=device, device_id_type=MESH)

    def greet_fluid(d, carry):
        signal((lax.rem(f + d, NF), s))
        return carry

    lax.fori_loop(1, NF, greet_fluid, 0)

    def greet_near(d, carry):
        signal(near_id(d)[1])
        return carry

    lax.fori_loop(1, 8, greet_near, 0)
    signal(nxt_id)
    signal(prv_id)

    def load(src, dst, i):
        copy = pltpu.make_async_copy(src, dst, lsem.at[i])
        copy.start()
        return copy

    part = POINTS // CHUNKS
    l_own = load(owner, ownv, 0)
    l_row = load(row, rowv, 1)
    l_v = load(vh, vv, 2)
    l_a = load(aop, av, 3)
    l_wc = load(wc, wcv, 4)
    l_ws = load(ws, wsv, 5)
    l_wm = load(wm, wmv, 6)
    l_disp = load(disp, dbuf.at[:, pl.ds(8, ROWS), :], 7)
    l_stiff = load(stiff, sbuf.at[pl.ds(8, ROWS), :], 8)
    l_flow = [
        load(flow.at[:, pl.ds(i * part, part), :], fbuf.at[:, pl.ds(EDGE + i * part, part), :], 9 + i)
        for i in range(CHUNKS)
    ]
    l_rbf = load(rbf, rbv, 9 + CHUNKS)
    l_w = load(wh, wv, 10 + CHUNKS)

    l_own.wait()
    l_row.wait()
    own_row = ownv[...].astype(F32)
    lab_row = rowv[...].astype(F32)
    eye = iota((HIST, HIST), 0) == iota((HIST, HIST), 1)
    ones = jnp.ones((BLOCKS, 128), BF16)
    own_col = dot(jnp.where(eye, own_row, 0.0).astype(BF16), ones)
    lab[...] = dot(jnp.where(eye, lab_row, 0.0).astype(BF16), ones) + 1.0
    same = own_col[:, :BLOCKS] == own_row
    above = iota((BLOCKS, BLOCKS), 0) < iota((BLOCKS, BLOCKS), 1)
    before_row = jnp.sum(jnp.where(same & above, 1.0, 0.0), axis=0, keepdims=True)
    below = iota((BLOCKS, BLOCKS), 1) < iota((BLOCKS, BLOCKS), 0)
    before_col = dot(jnp.where(same & below, 1.0, 0.0).astype(BF16), ones)
    both = jnp.where(iota((16, BLOCKS), 0) == 0, own_row, before_row).astype(BF16)
    wide = dot(both, jnp.where(iota((BLOCKS, 512), 1) // 8 == iota((BLOCKS, 512), 0), 1.0, 0.0).astype(BF16))

    def target(own, before, comp):
        return own * SLOTS + jnp.where(comp < 3.0, before * 3.0 + comp, jnp.where(comp == 3.0, 9.0 + before, -1e6))

    tgt_row = target(wide[0:1], wide[1:2], lax.rem(iota((1, 512), 1), 8).astype(F32))
    oh[...] = jnp.where(iota((512, 512), 0).astype(F32) == tgt_row, 1.0, 0.0).astype(BF16)
    tall = jnp.where(iota((512, BLOCKS), 0) // 8 == iota((512, BLOCKS), 1), 1.0, 0.0).astype(BF16)
    tgt_col = target(
        dot(tall, own_col.astype(BF16)),
        dot(tall, before_col.astype(BF16)),
        lax.rem(iota((512, 128), 0), 8).astype(F32),
    )
    for t in range(4):
        oht[:, t * 128 : (t + 1) * 128] = jnp.where(
            (iota((512, 128), 1) + t * 128).astype(F32) == tgt_col, 1.0, 0.0
        ).astype(BF16)

    l_v.wait()

    def history(i):
        return vv[pl.ds(i, HIST, stride=ENT), :]

    def gram_step(t, acc):
        for u in range(4):
            i = t * 8 + u * 2
            x = jnp.concatenate([history(i), history(i + 1)], axis=1)
            hi, lo = halves(x)
            acc = acc + dot_t(hi, jnp.concatenate([hi, lo], axis=0))
        return acc

    gram = lax.fori_loop(0, ENT // 8, gram_step, jnp.zeros((HIST, 128), F32))
    half = 0.5 * gram[:, :HIST] + gram[:, HIST:]
    packed = jnp.concatenate([half[:32], half[32:]], axis=1)
    gsend[...] = packed
    gin1[near] = packed

    pl.semaphore_wait(barrier, NF - 1 + 7 + 2)

    def send(src, dst, i, device):
        pltpu.make_async_remote_copy(
            src_ref=src, dst_ref=dst, send_sem=ssem.at[i], recv_sem=rsem.at[i],
            device_id=device, device_id_type=MESH,
        ).start()

    def taken(ref, sem):
        pltpu.make_async_copy(ref, ref, sem).wait()

    l_disp.wait()
    l_stiff.wait()
    send(flow.at[:, pl.ds(POINTS - EDGE, EDGE), :], fbuf.at[:, pl.ds(0, EDGE), :], 0, nxt_id)
    send(flow.at[:, pl.ds(0, EDGE), :], fbuf.at[:, pl.ds(EDGE + POINTS, EDGE), :], 1, prv_id)
    send(dbuf.at[:, pl.ds(ROWS, 8), :], dbuf.at[:, pl.ds(0, 8), :], 2, nxt_id)
    send(dbuf.at[:, pl.ds(8, 8), :], dbuf.at[:, pl.ds(ROWS + 8, 8), :], 3, prv_id)
    send(sbuf.at[pl.ds(ROWS, 8), :], sbuf.at[pl.ds(0, 8), :], 4, nxt_id)
    send(sbuf.at[pl.ds(8, 8), :], sbuf.at[pl.ds(ROWS + 8, 8), :], 5, prv_id)

    def reduce_near(src, dst, i):
        def step(d, carry):
            send(src, dst.at[near], i, near_id(d)[1])
            return carry

        lax.fori_loop(1, 8, step, 0)

    def reduce_far(src, dst, i):
        def step(d, carry):
            send(src, dst.at[chip], i, far_id(d)[1])
            return carry

        lax.fori_loop(1, 16, step, 0)

    reduce_near(gsend, gin1, 6)

    l_a.wait()
    l_wc.wait()
    l_ws.wait()
    l_wm.wait()
    l_rbf.wait()
    a = av[...]
    coupling = wcv[...]

    def slab(chunk):
        for u in range(8):
            base = pl.multiple_of((chunk * 8 + u) * BLK, BLK)
            for c in range(3):
                ext = fbuf[c, pl.ds(base, BLK + 2 * EDGE), :]
                e = wide32.at[u * 3 + c]
                e[...] = ext.astype(F32)
                near_by = e[pl.ds(EDGE - 1, BLK), :] + e[pl.ds(EDGE + 1, BLK), :]
                drift = dot(ext[EDGE : EDGE + BLK], a)
                motion = jnp.broadcast_to(wmv[c : c + 1, pl.ds(base, BLK)], (BLK, 128)).T
                new = 0.5 * e[pl.ds(EDGE, BLK), :] + 0.25 * near_by + drift + motion * coupling
                nf[c, pl.ds(base, BLK), :] = new.astype(BF16)

    def slab_step(i, carry):
        slab(i)
        return carry

    l_flow[0].wait()
    l_flow[1].wait()
    for i in range(1, CHUNKS - 1):
        if i == 4:
            taken(gin1.at[pl.ds(0, 7)], rsem.at[6])
            total = gin1[0]
            for g in range(1, 8):
                total = total + gin1[g]
            gsum1[...] = total
            gin2[chip] = total
            reduce_far(gsum1, gin2, 7)
        l_flow[i + 1].wait()
        lax.fori_loop(i, i + 1, slab_step, 0)
    taken(fbuf.at[:, pl.ds(0, EDGE), :], rsem.at[0])
    taken(fbuf.at[:, pl.ds(0, EDGE), :], rsem.at[1])

    @pl.when(me == 0)
    def _():
        fbuf[:, 0:EDGE, :] = jnp.zeros((3, EDGE, 128), BF16)

    @pl.when(me == ND - 1)
    def _():
        fbuf[:, EDGE + POINTS :, :] = jnp.zeros((3, EDGE, 128), BF16)

    def slab_edge(i, carry):
        slab(i * (CHUNKS - 1))
        return carry

    lax.fori_loop(0, 2, slab_edge, 0)

    stencil = jnp.concatenate([jnp.broadcast_to(wsv[...].astype(F32), (16, 128))] * 3, axis=1)
    stencil = jnp.where(iota((16, 384), 1) // 128 == iota((16, 384), 0), stencil, 0.0).astype(BF16)

    def pull(i, carry):
        base = pl.multiple_of(i * 16 * BLK, BLK)
        x = jnp.concatenate([nf[c, pl.ds(base, 16 * BLK), :] for c in range(3)], axis=1)
        t = dot_t(stencil, x).astype(BF16)
        for u in range(16):
            tract[i * 16 + u] = t[:, u * 128 : (u + 1) * 128]
        return carry

    lax.fori_loop(0, BLOCKS // 16, pull, 0)
    sub = iota((8, 128), 0)

    def spread_out(i, carry):
        for u in range(16):
            b = i * 16 + u
            m = dot(tract[b], rbv[b])[:8]
            m = jnp.where(sub < 3, m, jnp.where(sub == 3, lab[pl.ds(b, 1), :], 0.0))
            mapped[pl.ds(pl.multiple_of(b * 8, 8), 8), :] = m
        return carry

    lax.fori_loop(0, BLOCKS // 16, spread_out, 0)

    hi, lo = halves(mapped[...])
    out[...] = (dot(oh[...], hi) + dot(oh[...], lo)).reshape(NF, SLOTS, 128)

    def exchange(src, dst, i):
        def step(d, carry):
            other = lax.rem(f + d, NF)
            send(src.at[other], dst.at[f], i, (other, s))
            return carry

        lax.fori_loop(1, NF, step, 0)
        pltpu.make_async_copy(src.at[f], dst.at[f], rsem.at[i]).start()

    exchange(out, arrived, 8)

    taken(gin2.at[pl.ds(0, 15)], rsem.at[7])
    total = gin2[0]
    for g in range(1, 16):
        total = total + gin2[g]
    half = jnp.concatenate([total[:, :HIST], total[:, HIST:]], axis=0)
    work = jnp.concatenate([half + half.T, jnp.where(eye, 1.0, 0.0)], axis=1)
    sub64 = iota((HIST, 128), 0)

    def eliminate(work, first, last):
        for k in range(first, last):
            pivot = work[k : k + 1, :] * (1.0 / work[k : k + 1, k : k + 1])
            work = jnp.where(sub64 == k, pivot, work - work[:, k : k + 1] * pivot)
        return work

    work = eliminate(work, 0, 24)

    taken(arrived, rsem.at[8])
    got = arrived[...]
    slot = iota((NF, SLOTS, 128), 1)
    label = jnp.where(slot < 3, got[:, 9:10], jnp.where(slot < 6, got[:, 10:11], got[:, 11:12]))
    lane = iota((NF, SLOTS, 128), 2)
    hit = (label == (lax.rem(lane, ROWS) + 1).astype(F32)) & (lane // ROWS == lax.rem(slot, 3)) & (slot < 9)
    pt[...] = jnp.where(hit, 1.0, 0.0).astype(BF16).reshape(512, 128)
    hi, lo = halves(got.reshape(512, 128))
    place = pt[...]

    def placed(x):
        return lax.dot_general(place, x, (((0,), (0,)), ((), ())), preferred_element_type=F32)

    force = placed(hi) + placed(lo)
    fext[:, pl.ds(8, ROWS), :] = force[:ENT].reshape(3, ROWS, 128)
    send(fext.at[:, pl.ds(ROWS, 8), :], fext.at[:, pl.ds(0, 8), :], 9, nxt_id)
    send(fext.at[:, pl.ds(8, 8), :], fext.at[:, pl.ds(ROWS + 8, 8), :], 10, prv_id)

    work = eliminate(work, 24, 40)

    for i in (2, 3):
        taken(dbuf.at[:, pl.ds(0, 8), :], rsem.at[i])
    for i in (4, 5):
        taken(sbuf.at[pl.ds(0, 8), :], rsem.at[i])
    for i in (9, 10):
        taken(fext.at[:, pl.ds(0, 8), :], rsem.at[i])

    long = ROWS + 16
    at_row = iota((3, long, 128), 1) + me * ROWS - 8
    inside = (at_row >= 0) & (at_row < ND * ROWS)
    inverse = jnp.where(inside, 1.0 / (4.0 + sbuf[...])[None], 0.0)
    loads = jnp.where(inside, fext[...], 0.0)
    solved = jnp.where(inside, dbuf[...], 0.0)
    start = solved[:, 8 : 8 + ROWS]
    q = iota((3, long, 128), 2)
    for _ in range(SWEEPS):
        zero = jnp.zeros((3, 1, 128), F32)
        up = jnp.concatenate([zero, solved[:, : long - 1]], axis=1)
        down = jnp.concatenate([solved[:, 1:], zero], axis=1)
        left = jnp.where(q == 0, 0.0, pltpu.roll(solved, 1, 2))
        right = jnp.where(q == 127, 0.0, pltpu.roll(solved, 127, 2))
        solved = (loads + ((up + down) + (left + right))) * inverse
    solved = solved[:, 8 : 8 + ROWS]
    residual = (solved - start).reshape(ENT, 128)
    solved = solved.reshape(ENT, 128)

    resid[...] = residual

    def project(t, acc):
        for c in range(3):
            r8 = resid[pl.ds(pl.multiple_of(c * ROWS + t * 8, 8), 8), :]
            for u in range(8):
                acc = acc + history(c * ROWS + t * 8 + u) * r8[u : u + 1]
        return acc

    proj = lax.fori_loop(0, ROWS // 8, project, jnp.zeros((HIST, 128), F32))
    square = jnp.sum((residual * residual).reshape(ENT // 8, 8, 128), axis=0)
    sums = jnp.concatenate([proj, square, jnp.zeros((128 - HIST - 8, 128), F32)], axis=0)
    hi = sums.astype(BF16)
    rest = sums - hi.astype(F32)
    mid, low = halves(rest)
    one8 = jnp.ones((16, 128), BF16)
    line = (dot_t(one8, hi) + dot_t(one8, mid) + dot_t(one8, low))[:8]
    psend[...] = line
    pin1[near] = line
    reduce_near(psend, pin1, 11)

    work = eliminate(work, 40, 52)

    taken(pin1.at[pl.ds(0, 7)], rsem.at[11])
    total = pin1[0]
    for g in range(1, 8):
        total = total + pin1[g]
    psum1[...] = total
    pin2[chip] = total
    reduce_far(psum1, pin2, 12)

    work = eliminate(work, 52, 64)
    l_w.wait()

    taken(pin2.at[pl.ds(0, 15)], rsem.at[12])
    total = pin2[0]
    for g in range(1, 16):
        total = total + pin2[g]
    weights = -jnp.sum(work[:, HIST:] * total[0:1, :HIST], axis=1, keepdims=True)
    cbuf[...] = jnp.broadcast_to(weights, (HIST, 128))
    lane8 = iota((8, 128), 1)
    squares = jnp.sum(jnp.where((lane8 >= HIST) & (lane8 < HIST + 8), total, 0.0), axis=1, keepdims=True)
    norm[...] = jnp.sqrt(squares[0:1])

    def update(t, acc):
        for u in range(8):
            j = t * 8 + u
            acc = acc + cbuf[pl.ds(j, 1), :] * wv[pl.ds(pl.multiple_of(j * ENT, 8), ENT), :]
        return acc

    moved = solved + lax.fori_loop(0, HIST // 8, update, jnp.zeros((ENT, 128), F32))
    nd[...] = moved

    shell = jnp.concatenate([moved, jnp.zeros((128 - ENT, 128), F32)], axis=0).astype(BF16)
    rep[...] = dot(pt[...], shell).astype(BF16).reshape(NF, SLOTS, 128)
    exchange(rep, back, 13)
    taken(back, rsem.at[13])
    local[...] = dot(oht[...], back[...].reshape(512, 128)).astype(BF16)

    for i, ref in (
        (0, fbuf.at[:, pl.ds(0, EDGE), :]), (1, fbuf.at[:, pl.ds(0, EDGE), :]),
        (2, dbuf.at[:, pl.ds(0, 8), :]), (3, dbuf.at[:, pl.ds(0, 8), :]),
        (4, sbuf.at[pl.ds(0, 8), :]), (5, sbuf.at[pl.ds(0, 8), :]),
        (6, gin1.at[pl.ds(0, 7)]), (7, gin2.at[pl.ds(0, 15)]),
        (8, arrived.at[pl.ds(0, NF - 1)]),
        (9, fext.at[:, pl.ds(0, 8), :]), (10, fext.at[:, pl.ds(0, 8), :]),
        (11, pin1.at[pl.ds(0, 7)]), (12, pin2.at[pl.ds(0, 15)]),
        (13, back.at[pl.ds(0, NF - 1)]),
    ):
        taken(ref, ssem.at[i])


def finish(nf, nd, local, norm, rbv, nf_out, nd_out, wn, norm_out, sems):
    copies = []
    for k in range(3):
        copies.append(pltpu.make_async_copy(nf.at[k], nf_out.at[k], sems.at[k]))
    copies.append(pltpu.make_async_copy(nd, nd_out, sems.at[3]))
    copies.append(pltpu.make_async_copy(norm, norm_out, sems.at[4]))
    for copy in copies:
        copy.start()

    def wall(i, carry):
        for u in range(16):
            b = i * 16 + u
            rows = local[pl.ds(pl.multiple_of(b * 8, 8), 8), :]
            wn[:, pl.ds(pl.multiple_of(b * BLK, BLK), BLK)] = dot_t(rows, rbv[b])[:3]
        return carry

    lax.fori_loop(0, BLOCKS // 16, wall, 0)
    for copy in copies:
        copy.wait()


def per_device(flow, wm, aop, wc, ws, rbf, owner, row, disp, stiff, vh, wh):
    any_ = pl.BlockSpec(memory_space=pl.ANY)
    vmem = pl.BlockSpec(memory_space=pltpu.VMEM)
    out = pl.pallas_call(
        kernel,
        name="coupling",
        out_shape=(
            pltpu.VMEM((3, POINTS, 128), BF16),
            pltpu.VMEM((ENT, 128), F32),
            pltpu.VMEM((BLOCKS * 8, 128), BF16),
            pltpu.VMEM((1, 1), F32),
            pltpu.VMEM((BLOCKS, BLK, 128), BF16),
        ),
        in_specs=[pl.BlockSpec(memory_space=pltpu.HBM)] * 12,
        out_specs=(vmem,) * 5,
        scratch_shapes=[
            pltpu.VMEM((3, POINTS + 2 * EDGE, 128), BF16),
            pltpu.VMEM((3, POINTS), F32),
            pltpu.VMEM((128, 128), BF16),
            pltpu.VMEM((1, 128), F32),
            pltpu.VMEM((1, 128), BF16),
            pltpu.VMEM((1, BLOCKS), jnp.int32),
            pltpu.VMEM((1, BLOCKS), jnp.int32),
            pltpu.VMEM((3, ROWS + 16, 128), F32),
            pltpu.VMEM((ROWS + 16, 128), F32),
            pltpu.VMEM((HIST * ENT, 128), F32),
            pltpu.VMEM((HIST * ENT, 128), F32),
            pltpu.VMEM((BLOCKS * 8, 128), F32),
            pltpu.VMEM((512, 512), BF16),
            pltpu.VMEM((512, 512), BF16),
            pltpu.VMEM((BLOCKS, 128), F32),
            pltpu.VMEM((32, 128), F32),
            pltpu.VMEM((8, 32, 128), F32),
            pltpu.VMEM((32, 128), F32),
            pltpu.VMEM((16, 32, 128), F32),
            pltpu.VMEM((NF, SLOTS, 128), F32),
            pltpu.VMEM((NF, SLOTS, 128), F32),
            pltpu.VMEM((512, 128), BF16),
            pltpu.VMEM((3, ROWS + 16, 128), F32),
            pltpu.VMEM((8, 128), F32),
            pltpu.VMEM((8, 8, 128), F32),
            pltpu.VMEM((8, 128), F32),
            pltpu.VMEM((16, 8, 128), F32),
            pltpu.VMEM((HIST, 128), F32),
            pltpu.VMEM((NF, SLOTS, 128), BF16),
            pltpu.VMEM((NF, SLOTS, 128), BF16),
            pltpu.VMEM((ENT, 128), F32),
            pltpu.VMEM((24, BLK + 2 * EDGE, 128), F32),
            pltpu.VMEM((BLOCKS, 16, 128), BF16),
            pltpu.SemaphoreType.DMA((11 + CHUNKS,)),
            pltpu.SemaphoreType.DMA((14,)),
            pltpu.SemaphoreType.DMA((14,)),
        ],
        compiler_params=pltpu.CompilerParams(
            collective_id=0, has_side_effects=True, vmem_limit_bytes=55 << 20
        ),
    )(
        flow, wm, aop, wc.reshape(1, 128), ws.reshape(1, 128), rbf,
        owner.reshape(1, BLOCKS), row.reshape(1, BLOCKS),
        jnp.transpose(disp, (1, 0, 2)), stiff,
        jnp.transpose(vh, (0, 2, 1, 3)).reshape(HIST * ENT, 128),
        jnp.transpose(wh, (0, 2, 1, 3)).reshape(HIST * ENT, 128),
    )
    new_flow, moved, wall_next, norm = pl.pallas_call(
        finish,
        name="wall",
        out_shape=(
            jax.ShapeDtypeStruct((3, POINTS, 128), BF16),
            jax.ShapeDtypeStruct((ENT, 128), F32),
            jax.ShapeDtypeStruct((3, POINTS), F32),
            jax.ShapeDtypeStruct((1, 1), F32),
        ),
        in_specs=[vmem] * 5,
        out_specs=(any_, any_, vmem, any_),
        scratch_shapes=[pltpu.SemaphoreType.DMA((5,))],
        compiler_params=pltpu.CompilerParams(vmem_limit_bytes=8 << 20),
    )(*out)
    moved = jnp.transpose(moved.reshape(3, ROWS, 128), (1, 0, 2))
    return new_flow, moved, wall_next, norm.reshape(())


def solution(mesh):
    both = ("fluid", "solid")
    return jax.shard_map(
        per_device,
        mesh=mesh,
        in_specs=(
            P(None, both, None), P(None, both), P(), P(), P(), P(both, None, None), P(both, None), P(both, None),
            P(both, None, None), P(both, None), P(None, both, None, None), P(None, both, None, None),
        ),
        out_specs=(P(None, both, None), P(both, None, None), P(None, both), P()),
        check_vma=False,
    )
```

profile of v0, /device:TPU:1, one launch (start us, length us, event | category | flops | bytes accessed | tf_op | source)
XLA Modules:
  0.0 56.5 jit_solution(16043761442782042596)
XLA Ops:
  0.6 51.9 %coupling.1 = (bf16[3,8192,128]{2,1,0:T(8,128)(2,1)S(1)}, f32[96,128]{1,0:T(8,128)S(1)}, bf16[512,128]{1,0:T(8,128)(2,1)S(1)}, f32[1,1]{1,0:T(1,128)}, bf16[64,128,128]{2,1,0:T(8,128)(2,1)S(1)}) custom-call(bf16[3,8192,128]{2,1,0:T(8,128)(2,1)} %flow.1, f32[3,8192]{1,0:T(4,128)} %wm.1, bf16[128,128]{1,0:T(8,128)(2,1)} %aop.1, f32[1,128]{1,0:T(1,128)} %bitcast.18, ...), custom_call_target="tpu_custom_call" | custom-call | tf_op jit(solution)/shard_map/coupling/pallas_call | solution.py:445
  52.5 4.0 %wall.1 = (bf16[3,8192,128]{2,1,0:T(8,128)(2,1)}, f32[96,128]{1,0:T(8,128)}, f32[3,8192]{1,0:T(4,128)}, f32[1,1]{1,0:T(1,128)}) custom-call(bf16[3,8192,128]{2,1,0:T(8,128)(2,1)S(1)} %get-tuple-element.13.nf, f32[96,128]{1,0:T(8,128)S(1)} %get-tuple-element.14.nd, bf16[512,128]{1,0:T(8,128)(2,1)S(1)} %get-tuple-element.15.local, ...), custom_call_target="tpu_custom_call" | custom-call | tf_op jit(solution)/shard_map/wall/pallas_call | solution.py:505
where the time goes:
time: 56.7 us; the launch traced here: 56.5 us
  Pallas kernels  55.9 us (99%)
  between operations  0.64 us (1%)
    pallas_call x1, Pallas kernels, per_device(): pl.pallas_call(kernel, name='coupling', out_shape=(pltpu.VMEM((3, POINTS,...  51.9 us
    pallas_call x1, Pallas kernels, per_device(): pl.pallas_call(finish, name='wall', out_shape=(jax.ShapeDtypeStruct((3, P...  4.03 us

commit v1 on v0

--- a/solution.py
+++ b/solution.py
@@ -45,7 +45,7 @@
     nf, nd, local, norm, rbv,
     fbuf, wmv, av, wcv, wsv, ownv, rowv, dbuf, sbuf, vv, wv,
     mapped, oh, oht, lab, gsend, gin1, gsum1, gin2, out, arrived, pt, fext,
-    psend, pin1, psum1, pin2, cbuf, rep, back, resid, wide32, tract,
+    psend, pin, cbuf, rep, back, resid, wide32, tract,
     lsem, ssem, rsem,
 ):
     f, s = lax.axis_index("fluid"), lax.axis_index("solid")
@@ -195,40 +195,74 @@
     l_wc.wait()
     l_ws.wait()
     l_wm.wait()
-    l_rbf.wait()
     a = av[...]
     coupling = wcv[...]
 
-    def slab(chunk):
+    stencil = jnp.concatenate([jnp.broadcast_to(wsv[...].astype(F32), (16, 128))] * 3, axis=1)
+    stencil = jnp.where(iota((16, 384), 1) // 128 == iota((16, 384), 0), stencil, 0.0).astype(BF16)
+    sub = iota((8, 128), 0)
+
+    def slab(b, u):
+        base = pl.multiple_of(b * BLK, BLK)
+        for c in range(3):
+            ext = fbuf[c, pl.ds(base, BLK + 2 * EDGE), :]
+            e = wide32.at[u * 3 + c]
+            e[...] = ext.astype(F32)
+            near_by = e[pl.ds(EDGE - 1, BLK), :] + e[pl.ds(EDGE + 1, BLK), :]
+            drift = dot(ext[EDGE : EDGE + BLK], a)
+            motion = jnp.broadcast_to(wmv[c : c + 1, pl.ds(base, BLK)], (BLK, 128)).T
+            new = 0.5 * e[pl.ds(EDGE, BLK), :] + 0.25 * near_by + drift + motion * coupling
+            nf[c, pl.ds(base, BLK), :] = new.astype(BF16)
+
+    def slab_step(i, carry):
         for u in range(8):
-            base = pl.multiple_of((chunk * 8 + u) * BLK, BLK)
-            for c in range(3):
-                ext = fbuf[c, pl.ds(base, BLK + 2 * EDGE), :]
-                e = wide32.at[u * 3 + c]
-                e[...] = ext.astype(F32)
-                near_by = e[pl.ds(EDGE - 1, BLK), :] + e[pl.ds(EDGE + 1, BLK), :]
-                drift = dot(ext[EDGE : EDGE + BLK], a)
-                motion = jnp.broadcast_to(wmv[c : c + 1, pl.ds(base, BLK)], (BLK, 128)).T
-                new = 0.5 * e[pl.ds(EDGE, BLK), :] + 0.25 * near_by + drift + motion * coupling
-                nf[c, pl.ds(base, BLK), :] = new.astype(BF16)
-
-    def slab_step(i, carry):
-        slab(i)
-        return carry
-
+            slab(i * 8 + u, u)
+        return carry
+
+    def pull(points):
+        x = jnp.concatenate([nf[c, points, :] for c in range(3)], axis=1)
+        return dot_t(stencil, x).astype(BF16)
+
+    def spread_out(b, tractions):
+        m = dot(tractions, rbv[b])[:8]
+        m = jnp.where(sub < 3, m, jnp.where(sub == 3, lab[pl.ds(b, 1), :], 0.0))
+        mapped[pl.ds(pl.multiple_of(b * 8, 8), 8), :] = m
+
+    def pull_step(i, carry):
+        t = pull(pl.ds(pl.multiple_of(i * 16 * BLK, BLK), 16 * BLK))
+        for u in range(16):
+            tract[i * 16 + u] = t[:, u * 128 : (u + 1) * 128]
+        return carry
+
+    def map_step(i, carry):
+        for u in range(16):
+            spread_out(i * 16 + u, tract[i * 16 + u])
+        return carry
+
+    ends = (0, BLOCKS - 1)
+    for b in ends:
+        nf[:, b * BLK : (b + 1) * BLK, :] = jnp.zeros((3, BLK, 128), BF16)
     l_flow[0].wait()
     l_flow[1].wait()
+    for u in range(1, 8):
+        slab(u, u)
     for i in range(1, CHUNKS - 1):
-        if i == 4:
-            taken(gin1.at[pl.ds(0, 7)], rsem.at[6])
-            total = gin1[0]
-            for g in range(1, 8):
-                total = total + gin1[g]
-            gsum1[...] = total
-            gin2[chip] = total
-            reduce_far(gsum1, gin2, 7)
         l_flow[i + 1].wait()
         lax.fori_loop(i, i + 1, slab_step, 0)
+    for u in range(7):
+        slab(BLOCKS - 8 + u, u)
+    l_rbf.wait()
+    lax.fori_loop(0, BLOCKS // 16, pull_step, 0)
+    lax.fori_loop(0, BLOCKS // 16, map_step, 0)
+
+    taken(gin1.at[pl.ds(0, 7)], rsem.at[6])
+    total = gin1[0]
+    for g in range(1, 8):
+        total = total + gin1[g]
+    gsum1[...] = total
+    gin2[chip] = total
+    reduce_far(gsum1, gin2, 7)
+
     taken(fbuf.at[:, pl.ds(0, EDGE), :], rsem.at[0])
     taken(fbuf.at[:, pl.ds(0, EDGE), :], rsem.at[1])
 
@@ -240,35 +274,10 @@
     def _():
         fbuf[:, EDGE + POINTS :, :] = jnp.zeros((3, EDGE, 128), BF16)
 
-    def slab_edge(i, carry):
-        slab(i * (CHUNKS - 1))
-        return carry
-
-    lax.fori_loop(0, 2, slab_edge, 0)
-
-    stencil = jnp.concatenate([jnp.broadcast_to(wsv[...].astype(F32), (16, 128))] * 3, axis=1)
-    stencil = jnp.where(iota((16, 384), 1) // 128 == iota((16, 384), 0), stencil, 0.0).astype(BF16)
-
-    def pull(i, carry):
-        base = pl.multiple_of(i * 16 * BLK, BLK)
-        x = jnp.concatenate([nf[c, pl.ds(base, 16 * BLK), :] for c in range(3)], axis=1)
-        t = dot_t(stencil, x).astype(BF16)
-        for u in range(16):
-            tract[i * 16 + u] = t[:, u * 128 : (u + 1) * 128]
-        return carry
-
-    lax.fori_loop(0, BLOCKS // 16, pull, 0)
-    sub = iota((8, 128), 0)
-
-    def spread_out(i, carry):
-        for u in range(16):
-            b = i * 16 + u
-            m = dot(tract[b], rbv[b])[:8]
-            m = jnp.where(sub < 3, m, jnp.where(sub == 3, lab[pl.ds(b, 1), :], 0.0))
-            mapped[pl.ds(pl.multiple_of(b * 8, 8), 8), :] = m
-        return carry
-
-    lax.fori_loop(0, BLOCKS // 16, spread_out, 0)
+    for u, b in enumerate(ends):
+        slab(b, u)
+    for b in ends:
+        spread_out(b, pull(pl.ds(b * BLK, BLK)))
 
     hi, lo = halves(mapped[...])
     out[...] = (dot(oh[...], hi) + dot(oh[...], lo)).reshape(NF, SLOTS, 128)
@@ -283,22 +292,6 @@
         pltpu.make_async_copy(src.at[f], dst.at[f], rsem.at[i]).start()
 
     exchange(out, arrived, 8)
-
-    taken(gin2.at[pl.ds(0, 15)], rsem.at[7])
-    total = gin2[0]
-    for g in range(1, 16):
-        total = total + gin2[g]
-    half = jnp.concatenate([total[:, :HIST], total[:, HIST:]], axis=0)
-    work = jnp.concatenate([half + half.T, jnp.where(eye, 1.0, 0.0)], axis=1)
-    sub64 = iota((HIST, 128), 0)
-
-    def eliminate(work, first, last):
-        for k in range(first, last):
-            pivot = work[k : k + 1, :] * (1.0 / work[k : k + 1, k : k + 1])
-            work = jnp.where(sub64 == k, pivot, work - work[:, k : k + 1] * pivot)
-        return work
-
-    work = eliminate(work, 0, 24)
 
     taken(arrived, rsem.at[8])
     got = arrived[...]
@@ -318,7 +311,21 @@
     send(fext.at[:, pl.ds(ROWS, 8), :], fext.at[:, pl.ds(0, 8), :], 9, nxt_id)
     send(fext.at[:, pl.ds(8, 8), :], fext.at[:, pl.ds(ROWS + 8, 8), :], 10, prv_id)
 
-    work = eliminate(work, 24, 40)
+    taken(gin2.at[pl.ds(0, 15)], rsem.at[7])
+    total = gin2[0]
+    for g in range(1, 16):
+        total = total + gin2[g]
+    half = jnp.concatenate([total[:, :HIST], total[:, HIST:]], axis=0)
+    work = jnp.concatenate([half + half.T, jnp.where(eye, 1.0, 0.0)], axis=1)
+    sub64 = iota((HIST, 128), 0)
+
+    def eliminate(work, first, last):
+        for k in range(first, last):
+            pivot = work[k : k + 1, :] * (1.0 / work[k : k + 1, k : k + 1])
+            work = jnp.where(sub64 == k, pivot, work - work[:, k : k + 1] * pivot)
+        return work
+
+    work = eliminate(work, 0, 28)
 
     for i in (2, 3):
         taken(dbuf.at[:, pl.ds(0, 8), :], rsem.at[i])
@@ -348,47 +355,42 @@
 
     resid[...] = residual
 
-    def project(t, acc):
-        for c in range(3):
-            r8 = resid[pl.ds(pl.multiple_of(c * ROWS + t * 8, 8), 8), :]
-            for u in range(8):
-                acc = acc + history(c * ROWS + t * 8 + u) * r8[u : u + 1]
-        return acc
-
-    proj = lax.fori_loop(0, ROWS // 8, project, jnp.zeros((HIST, 128), F32))
+    def project(t, accs):
+        accs = list(accs)
+        for u in range(48):
+            i = t * 48 + u
+            accs[u % 4] = accs[u % 4] + history(i) * resid[pl.ds(i, 1), :]
+        return tuple(accs)
+
+    accs = lax.fori_loop(0, 2, project, (jnp.zeros((HIST, 128), F32),) * 4)
+    proj = (accs[0] + accs[1]) + (accs[2] + accs[3])
     square = jnp.sum((residual * residual).reshape(ENT // 8, 8, 128), axis=0)
     sums = jnp.concatenate([proj, square, jnp.zeros((128 - HIST - 8, 128), F32)], axis=0)
     hi = sums.astype(BF16)
     rest = sums - hi.astype(F32)
     mid, low = halves(rest)
     one8 = jnp.ones((16, 128), BF16)
-    line = (dot_t(one8, hi) + dot_t(one8, mid) + dot_t(one8, low))[:8]
+    line = (dot_t(one8, hi) + dot_t(one8, mid) + dot_t(one8, low))[:1]
     psend[...] = line
-    pin1[near] = line
-    reduce_near(psend, pin1, 11)
-
-    work = eliminate(work, 40, 52)
-
-    taken(pin1.at[pl.ds(0, 7)], rsem.at[11])
-    total = pin1[0]
-    for g in range(1, 8):
-        total = total + pin1[g]
-    psum1[...] = total
-    pin2[chip] = total
-    reduce_far(psum1, pin2, 12)
-
-    work = eliminate(work, 52, 64)
+    pin[me] = line
+
+    def tell(d, carry):
+        other = lax.rem(me + d, ND)
+        send(psend, pin.at[me], 11, (other // NS, lax.rem(other, NS)))
+        return carry
+
+    lax.fori_loop(1, ND, tell, 0)
+
+    work = eliminate(work, 28, 64)
     l_w.wait()
 
-    taken(pin2.at[pl.ds(0, 15)], rsem.at[12])
-    total = pin2[0]
-    for g in range(1, 16):
-        total = total + pin2[g]
+    taken(pin.at[pl.ds(0, ND - 1)], rsem.at[11])
+    total = jnp.sum(pin[...], axis=0)
     weights = -jnp.sum(work[:, HIST:] * total[0:1, :HIST], axis=1, keepdims=True)
     cbuf[...] = jnp.broadcast_to(weights, (HIST, 128))
-    lane8 = iota((8, 128), 1)
-    squares = jnp.sum(jnp.where((lane8 >= HIST) & (lane8 < HIST + 8), total, 0.0), axis=1, keepdims=True)
-    norm[...] = jnp.sqrt(squares[0:1])
+    lane1 = iota((1, 128), 1)
+    squares = jnp.sum(jnp.where((lane1 >= HIST) & (lane1 < HIST + 8), total, 0.0), axis=1, keepdims=True)
+    norm[...] = jnp.sqrt(squares)
 
     def update(t, acc):
         for u in range(8):
@@ -401,8 +403,8 @@
 
     shell = jnp.concatenate([moved, jnp.zeros((128 - ENT, 128), F32)], axis=0).astype(BF16)
     rep[...] = dot(pt[...], shell).astype(BF16).reshape(NF, SLOTS, 128)
-    exchange(rep, back, 13)
-    taken(back, rsem.at[13])
+    exchange(rep, back, 12)
+    taken(back, rsem.at[12])
     local[...] = dot(oht[...], back[...].reshape(512, 128)).astype(BF16)
 
     for i, ref in (
@@ -412,8 +414,8 @@
         (6, gin1.at[pl.ds(0, 7)]), (7, gin2.at[pl.ds(0, 15)]),
         (8, arrived.at[pl.ds(0, NF - 1)]),
         (9, fext.at[:, pl.ds(0, 8), :]), (10, fext.at[:, pl.ds(0, 8), :]),
-        (11, pin1.at[pl.ds(0, 7)]), (12, pin2.at[pl.ds(0, 15)]),
-        (13, back.at[pl.ds(0, NF - 1)]),
+        (11, pin.at[pl.ds(0, ND - 1)]),
+        (12, back.at[pl.ds(0, NF - 1)]),
     ):
         taken(ref, ssem.at[i])
 
@@ -478,10 +480,8 @@
             pltpu.VMEM((NF, SLOTS, 128), F32),
             pltpu.VMEM((512, 128), BF16),
             pltpu.VMEM((3, ROWS + 16, 128), F32),
-            pltpu.VMEM((8, 128), F32),
-            pltpu.VMEM((8, 8, 128), F32),
-            pltpu.VMEM((8, 128), F32),
-            pltpu.VMEM((16, 8, 128), F32),
+            pltpu.VMEM((1, 128), F32),
+            pltpu.VMEM((ND, 1, 128), F32),
             pltpu.VMEM((HIST, 128), F32),
             pltpu.VMEM((NF, SLOTS, 128), BF16),
             pltpu.VMEM((NF, SLOTS, 128), BF16),
@@ -489,8 +489,8 @@
             pltpu.VMEM((24, BLK + 2 * EDGE, 128), F32),
             pltpu.VMEM((BLOCKS, 16, 128), BF16),
             pltpu.SemaphoreType.DMA((11 + CHUNKS,)),
-            pltpu.SemaphoreType.DMA((14,)),
-            pltpu.SemaphoreType.DMA((14,)),
+            pltpu.SemaphoreType.DMA((13,)),
+            pltpu.SemaphoreType.DMA((13,)),
         ],
         compiler_params=pltpu.CompilerParams(
             collective_id=0, has_side_effects=True, vmem_limit_bytes=55 << 20

time: 56.7 us -> 54.5 us (0.961)
  Pallas kernels: 55.9 us -> 53.7 us
    pallas_call x1, Pallas kernels: 51.9 us -> 49.7 us  [per_device(): pl.pallas_call(kernel, name='coupling', out_shape=(pltpu.VMEM((3, POINTS,...]
where the time goes in v1:
time: 54.5 us; the launch traced here: 54.4 us
  Pallas kernels  53.7 us (99%)
  between operations  0.64 us (1%)
    pallas_call x1, Pallas kernels, per_device(): pl.pallas_call(kernel, name='coupling', out_shape=(pltpu.VMEM((3, POINTS,...  49.7 us
    pallas_call x1, Pallas kernels, per_device(): pl.pallas_call(finish, name='wall', out_shape=(jax.ShapeDtypeStruct((3, P...  4.03 us

profile of v1, /device:TPU:1, one launch (start us, length us, event | category | flops | bytes accessed | tf_op | source)
XLA Modules:
  0.0 54.4 jit_solution(4671071652723946870)
XLA Ops:
  0.6 49.7 %coupling.1 = (bf16[3,8192,128]{2,1,0:T(8,128)(2,1)S(1)}, f32[96,128]{1,0:T(8,128)S(1)}, bf16[512,128]{1,0:T(8,128)(2,1)S(1)}, f32[1,1]{1,0:T(1,128)}, bf16[64,128,128]{2,1,0:T(8,128)(2,1)S(1)}) custom-call(bf16[3,8192,128]{2,1,0:T(8,128)(2,1)} %flow.1, f32[3,8192]{1,0:T(4,128)} %wm.1, bf16[128,128]{1,0:T(8,128)(2,1)} %aop.1, f32[1,128]{1,0:T(1,128)} %bitcast.18, ...), custom_call_target="tpu_custom_call" | custom-call | tf_op jit(solution)/shard_map/coupling/pallas_call | solution.py:447
  50.3 4.0 %wall.1 = (bf16[3,8192,128]{2,1,0:T(8,128)(2,1)}, f32[96,128]{1,0:T(8,128)}, f32[3,8192]{1,0:T(4,128)}, f32[1,1]{1,0:T(1,128)}) custom-call(bf16[3,8192,128]{2,1,0:T(8,128)(2,1)S(1)} %get-tuple-element.13.nf, f32[96,128]{1,0:T(8,128)S(1)} %get-tuple-element.14.nd, bf16[512,128]{1,0:T(8,128)(2,1)S(1)} %get-tuple-element.15.local, ...), custom_call_target="tpu_custom_call" | custom-call | tf_op jit(solution)/shard_map/wall/pallas_call | solution.py:505

commit v2 on v1

--- a/solution.py
+++ b/solution.py
@@ -88,21 +88,118 @@
         return copy
 
     part = POINTS // CHUNKS
-    l_own = load(owner, ownv, 0)
-    l_row = load(row, rowv, 1)
-    l_v = load(vh, vv, 2)
     l_a = load(aop, av, 3)
     l_wc = load(wc, wcv, 4)
     l_ws = load(ws, wsv, 5)
     l_wm = load(wm, wmv, 6)
-    l_disp = load(disp, dbuf.at[:, pl.ds(8, ROWS), :], 7)
-    l_stiff = load(stiff, sbuf.at[pl.ds(8, ROWS), :], 8)
     l_flow = [
         load(flow.at[:, pl.ds(i * part, part), :], fbuf.at[:, pl.ds(EDGE + i * part, part), :], 9 + i)
         for i in range(CHUNKS)
     ]
+    l_own = load(owner, ownv, 0)
+    l_row = load(row, rowv, 1)
+    l_disp = load(disp, dbuf.at[:, pl.ds(8, ROWS), :], 7)
+    l_stiff = load(stiff, sbuf.at[pl.ds(8, ROWS), :], 8)
     l_rbf = load(rbf, rbv, 9 + CHUNKS)
+    l_v = load(vh, vv, 2)
     l_w = load(wh, wv, 10 + CHUNKS)
+
+    def send(src, dst, i, device):
+        pltpu.make_async_remote_copy(
+            src_ref=src, dst_ref=dst, send_sem=ssem.at[i], recv_sem=rsem.at[i],
+            device_id=device, device_id_type=MESH,
+        ).start()
+
+    def taken(ref, sem):
+        pltpu.make_async_copy(ref, ref, sem).wait()
+
+    def reduce_near(src, dst, i):
+        def step(d, carry):
+            send(src, dst.at[near], i, near_id(d)[1])
+            return carry
+
+        lax.fori_loop(1, 8, step, 0)
+
+    def reduce_far(src, dst, i):
+        def step(d, carry):
+            send(src, dst.at[chip], i, far_id(d)[1])
+            return carry
+
+        lax.fori_loop(1, 16, step, 0)
+
+    l_a.wait()
+    l_wc.wait()
+    l_ws.wait()
+    l_wm.wait()
+    a = av[...]
+    coupling = wcv[...]
+
+    stencil = jnp.concatenate([jnp.broadcast_to(wsv[...].astype(F32), (16, 128))] * 3, axis=1)
+    stencil = jnp.where(iota((16, 384), 1) // 128 == iota((16, 384), 0), stencil, 0.0).astype(BF16)
+    sub = iota((8, 128), 0)
+
+    def slab(b, u):
+        base = pl.multiple_of(b * BLK, BLK)
+        for c in range(3):
+            ext = fbuf[c, pl.ds(base, BLK + 2 * EDGE), :]
+            e = wide32.at[u * 3 + c]
+            e[...] = ext.astype(F32)
+            near_by = e[pl.ds(EDGE - 1, BLK), :] + e[pl.ds(EDGE + 1, BLK), :]
+            drift = dot(ext[EDGE : EDGE + BLK], a)
+            motion = jnp.broadcast_to(wmv[c : c + 1, pl.ds(base, BLK)], (BLK, 128)).T
+            new = 0.5 * e[pl.ds(EDGE, BLK), :] + 0.25 * near_by + drift + motion * coupling
+            nf[c, pl.ds(base, BLK), :] = new.astype(BF16)
+
+    def slab_step(i, carry):
+        for u in range(8):
+            slab(i * 8 + u, u)
+        return carry
+
+    def pull(points):
+        x = jnp.concatenate([nf[c, points, :] for c in range(3)], axis=1)
+        return dot_t(stencil, x).astype(BF16)
+
+    def spread_out(b, tractions):
+        m = dot(tractions, rbv[b])[:8]
+        m = jnp.where(sub < 3, m, jnp.where(sub == 3, lab[pl.ds(b, 1), :], 0.0))
+        mapped[pl.ds(pl.multiple_of(b * 8, 8), 8), :] = m
+
+    def pull_step(i, carry):
+        t = pull(pl.ds(pl.multiple_of(i * 16 * BLK, BLK), 16 * BLK))
+        for u in range(16):
+            tract[i * 16 + u] = t[:, u * 128 : (u + 1) * 128]
+        return carry
+
+    def map_step(i, carry):
+        for u in range(16):
+            spread_out(i * 16 + u, tract[i * 16 + u])
+        return carry
+
+    ends = (0, BLOCKS - 1)
+    for b in ends:
+        nf[:, b * BLK : (b + 1) * BLK, :] = jnp.zeros((3, BLK, 128), BF16)
+    l_flow[0].wait()
+    l_flow[1].wait()
+    for u in range(1, 8):
+        slab(u, u)
+    for i in range(1, CHUNKS - 1):
+        l_flow[i + 1].wait()
+        lax.fori_loop(i, i + 1, slab_step, 0)
+    for u in range(7):
+        slab(BLOCKS - 8 + u, u)
+
+    pl.semaphore_wait(barrier, NF - 1 + 7 + 2)
+
+    l_disp.wait()
+    l_stiff.wait()
+    send(flow.at[:, pl.ds(POINTS - EDGE, EDGE), :], fbuf.at[:, pl.ds(0, EDGE), :], 0, nxt_id)
+    send(flow.at[:, pl.ds(0, EDGE), :], fbuf.at[:, pl.ds(EDGE + POINTS, EDGE), :], 1, prv_id)
+    send(dbuf.at[:, pl.ds(ROWS, 8), :], dbuf.at[:, pl.ds(0, 8), :], 2, nxt_id)
+    send(dbuf.at[:, pl.ds(8, 8), :], dbuf.at[:, pl.ds(ROWS + 8, 8), :], 3, prv_id)
+    send(sbuf.at[pl.ds(ROWS, 8), :], sbuf.at[pl.ds(0, 8), :], 4, nxt_id)
+    send(sbuf.at[pl.ds(8, 8), :], sbuf.at[pl.ds(ROWS + 8, 8), :], 5, prv_id)
+
+    lax.fori_loop(0, BLOCKS // 16, pull_step, 0)
 
     l_own.wait()
     l_row.wait()
@@ -136,6 +233,39 @@
             (iota((512, 128), 1) + t * 128).astype(F32) == tgt_col, 1.0, 0.0
         ).astype(BF16)
 
+    l_rbf.wait()
+    lax.fori_loop(0, BLOCKS // 16, map_step, 0)
+
+    taken(fbuf.at[:, pl.ds(0, EDGE), :], rsem.at[0])
+    taken(fbuf.at[:, pl.ds(0, EDGE), :], rsem.at[1])
+
+    @pl.when(me == 0)
+    def _():
+        fbuf[:, 0:EDGE, :] = jnp.zeros((3, EDGE, 128), BF16)
+
+    @pl.when(me == ND - 1)
+    def _():
+        fbuf[:, EDGE + POINTS :, :] = jnp.zeros((3, EDGE, 128), BF16)
+
+    for u, b in enumerate(ends):
+        slab(b, u)
+    for b in ends:
+        spread_out(b, pull(pl.ds(b * BLK, BLK)))
+
+    hi, lo = halves(mapped[...])
+    out[...] = (dot(oh[...], hi) + dot(oh[...], lo)).reshape(NF, SLOTS, 128)
+
+    def exchange(src, dst, i):
+        def step(d, carry):
+            other = lax.rem(f + d, NF)
+            send(src.at[other], dst.at[f], i, (other, s))
+            return carry
+
+        lax.fori_loop(1, NF, step, 0)
+        pltpu.make_async_copy(src.at[f], dst.at[f], rsem.at[i]).start()
+
+    exchange(out, arrived, 8)
+
     l_v.wait()
 
     def history(i):
@@ -154,144 +284,7 @@
     packed = jnp.concatenate([half[:32], half[32:]], axis=1)
     gsend[...] = packed
     gin1[near] = packed
-
-    pl.semaphore_wait(barrier, NF - 1 + 7 + 2)
-
-    def send(src, dst, i, device):
-        pltpu.make_async_remote_copy(
-            src_ref=src, dst_ref=dst, send_sem=ssem.at[i], recv_sem=rsem.at[i],
-            device_id=device, device_id_type=MESH,
-        ).start()
-
-    def taken(ref, sem):
-        pltpu.make_async_copy(ref, ref, sem).wait()
-
-    l_disp.wait()
-    l_stiff.wait()
-    send(flow.at[:, pl.ds(POINTS - EDGE, EDGE), :], fbuf.at[:, pl.ds(0, EDGE), :], 0, nxt_id)
-    send(flow.at[:, pl.ds(0, EDGE), :], fbuf.at[:, pl.ds(EDGE + POINTS, EDGE), :], 1, prv_id)
-    send(dbuf.at[:, pl.ds(ROWS, 8), :], dbuf.at[:, pl.ds(0, 8), :], 2, nxt_id)
-    send(dbuf.at[:, pl.ds(8, 8), :], dbuf.at[:, pl.ds(ROWS + 8, 8), :], 3, prv_id)
-    send(sbuf.at[pl.ds(ROWS, 8), :], sbuf.at[pl.ds(0, 8), :], 4, nxt_id)
-    send(sbuf.at[pl.ds(8, 8), :], sbuf.at[pl.ds(ROWS + 8, 8), :], 5, prv_id)
-
-    def reduce_near(src, dst, i):
-        def step(d, carry):
-            send(src, dst.at[near], i, near_id(d)[1])
-            return carry
-
-        lax.fori_loop(1, 8, step, 0)
-
-    def reduce_far(src, dst, i):
-        def step(d, carry):
-            send(src, dst.at[chip], i, far_id(d)[1])
-            return carry
-
-        lax.fori_loop(1, 16, step, 0)
-
     reduce_near(gsend, gin1, 6)
-
-    l_a.wait()
-    l_wc.wait()
-    l_ws.wait()
-    l_wm.wait()
-    a = av[...]
-    coupling = wcv[...]
-
-    stencil = jnp.concatenate([jnp.broadcast_to(wsv[...].astype(F32), (16, 128))] * 3, axis=1)
-    stencil = jnp.where(iota((16, 384), 1) // 128 == iota((16, 384), 0), stencil, 0.0).astype(BF16)
-    sub = iota((8, 128), 0)
-
-    def slab(b, u):
-        base = pl.multiple_of(b * BLK, BLK)
-        for c in range(3):
-            ext = fbuf[c, pl.ds(base, BLK + 2 * EDGE), :]
-            e = wide32.at[u * 3 + c]
-            e[...] = ext.astype(F32)
-            near_by = e[pl.ds(EDGE - 1, BLK), :] + e[pl.ds(EDGE + 1, BLK), :]
-            drift = dot(ext[EDGE : EDGE + BLK], a)
-            motion = jnp.broadcast_to(wmv[c : c + 1, pl.ds(base, BLK)], (BLK, 128)).T
-            new = 0.5 * e[pl.ds(EDGE, BLK), :] + 0.25 * near_by + drift + motion * coupling
-            nf[c, pl.ds(base, BLK), :] = new.astype(BF16)
-
-    def slab_step(i, carry):
-        for u in range(8):
-            slab(i * 8 + u, u)
-        return carry
-
-    def pull(points):
-        x = jnp.concatenate([nf[c, points, :] for c in range(3)], axis=1)
-        return dot_t(stencil, x).astype(BF16)
-
-    def spread_out(b, tractions):
-        m = dot(tractions, rbv[b])[:8]
-        m = jnp.where(sub < 3, m, jnp.where(sub == 3, lab[pl.ds(b, 1), :], 0.0))
-        mapped[pl.ds(pl.multiple_of(b * 8, 8), 8), :] = m
-
-    def pull_step(i, carry):
-        t = pull(pl.ds(pl.multiple_of(i * 16 * BLK, BLK), 16 * BLK))
-        for u in range(16):
-            tract[i * 16 + u] = t[:, u * 128 : (u + 1) * 128]
-        return carry
-
-    def map_step(i, carry):
-        for u in range(16):
-            spread_out(i * 16 + u, tract[i * 16 + u])
-        return carry
-
-    ends = (0, BLOCKS - 1)
-    for b in ends:
-        nf[:, b * BLK : (b + 1) * BLK, :] = jnp.zeros((3, BLK, 128), BF16)
-    l_flow[0].wait()
-    l_flow[1].wait()
-    for u in range(1, 8):
-        slab(u, u)
-    for i in range(1, CHUNKS - 1):
-        l_flow[i + 1].wait()
-        lax.fori_loop(i, i + 1, slab_step, 0)
-    for u in range(7):
-        slab(BLOCKS - 8 + u, u)
-    l_rbf.wait()
-    lax.fori_loop(0, BLOCKS // 16, pull_step, 0)
-    lax.fori_loop(0, BLOCKS // 16, map_step, 0)
-
-    taken(gin1.at[pl.ds(0, 7)], rsem.at[6])
-    total = gin1[0]
-    for g in range(1, 8):
-        total = total + gin1[g]
-    gsum1[...] = total
-    gin2[chip] = total
-    reduce_far(gsum1, gin2, 7)
-
-    taken(fbuf.at[:, pl.ds(0, EDGE), :], rsem.at[0])
-    taken(fbuf.at[:, pl.ds(0, EDGE), :], rsem.at[1])
-
-    @pl.when(me == 0)
-    def _():
-        fbuf[:, 0:EDGE, :] = jnp.zeros((3, EDGE, 128), BF16)
-
-    @pl.when(me == ND - 1)
-    def _():
-        fbuf[:, EDGE + POINTS :, :] = jnp.zeros((3, EDGE, 128), BF16)
-
-    for u, b in enumerate(ends):
-        slab(b, u)
-    for b in ends:
-        spread_out(b, pull(pl.ds(b * BLK, BLK)))
-
-    hi, lo = halves(mapped[...])
-    out[...] = (dot(oh[...], hi) + dot(oh[...], lo)).reshape(NF, SLOTS, 128)
-
-    def exchange(src, dst, i):
-        def step(d, carry):
-            other = lax.rem(f + d, NF)
-            send(src.at[other], dst.at[f], i, (other, s))
-            return carry
-
-        lax.fori_loop(1, NF, step, 0)
-        pltpu.make_async_copy(src.at[f], dst.at[f], rsem.at[i]).start()
-
-    exchange(out, arrived, 8)
 
     taken(arrived, rsem.at[8])
     got = arrived[...]
@@ -311,21 +304,13 @@
     send(fext.at[:, pl.ds(ROWS, 8), :], fext.at[:, pl.ds(0, 8), :], 9, nxt_id)
     send(fext.at[:, pl.ds(8, 8), :], fext.at[:, pl.ds(ROWS + 8, 8), :], 10, prv_id)
 
-    taken(gin2.at[pl.ds(0, 15)], rsem.at[7])
-    total = gin2[0]
-    for g in range(1, 16):
-        total = total + gin2[g]
-    half = jnp.concatenate([total[:, :HIST], total[:, HIST:]], axis=0)
-    work = jnp.concatenate([half + half.T, jnp.where(eye, 1.0, 0.0)], axis=1)
-    sub64 = iota((HIST, 128), 0)
-
-    def eliminate(work, first, last):
-        for k in range(first, last):
-            pivot = work[k : k + 1, :] * (1.0 / work[k : k + 1, k : k + 1])
-            work = jnp.where(sub64 == k, pivot, work - work[:, k : k + 1] * pivot)
-        return work
-
-    work = eliminate(work, 0, 28)
+    taken(gin1.at[pl.ds(0, 7)], rsem.at[6])
+    total = gin1[0]
+    for g in range(1, 8):
+        total = total + gin1[g]
+    gsum1[...] = total
+    gin2[chip] = total
+    reduce_far(gsum1, gin2, 7)
 
     for i in (2, 3):
         taken(dbuf.at[:, pl.ds(0, 8), :], rsem.at[i])
@@ -381,7 +366,20 @@
 
     lax.fori_loop(1, ND, tell, 0)
 
-    work = eliminate(work, 28, 64)
+    taken(gin2.at[pl.ds(0, 15)], rsem.at[7])
+    total = gin2[0]
+    for g in range(1, 16):
+        total = total + gin2[g]
+    half = jnp.concatenate([total[:, :HIST], total[:, HIST:]], axis=0)
+    work = jnp.concatenate([half + half.T, jnp.where(eye, 1.0, 0.0)], axis=1)
+    sub64 = iota((HIST, 128), 0)
+
+    def eliminate(work, first, last):
+        for k in range(first, last):
+            pivot = work[k : k + 1, :] * (1.0 / work[k : k + 1, k : k + 1])
+            work = jnp.where(sub64 == k, pivot, work - work[:, k : k + 1] * pivot)
+        return work
+    work = eliminate(work, 0, HIST)
     l_w.wait()
 
     taken(pin.at[pl.ds(0, ND - 1)], rsem.at[11])
@@ -420,23 +418,19 @@
         taken(ref, ssem.at[i])
 
 
-def finish(nf, nd, local, norm, rbv, nf_out, nd_out, wn, norm_out, sems):
-    copies = []
-    for k in range(3):
-        copies.append(pltpu.make_async_copy(nf.at[k], nf_out.at[k], sems.at[k]))
+def finish(nf, nd, local, norm, rbv, nf_out, nd_out, wn_out, norm_out, wn, sems):
+    copies = [pltpu.make_async_copy(nf.at[k], nf_out.at[k], sems.at[k]) for k in range(3)]
     copies.append(pltpu.make_async_copy(nd, nd_out, sems.at[3]))
     copies.append(pltpu.make_async_copy(norm, norm_out, sems.at[4]))
     for copy in copies:
         copy.start()
-
-    def wall(i, carry):
+    for i in range(4):
         for u in range(16):
             b = i * 16 + u
-            rows = local[pl.ds(pl.multiple_of(b * 8, 8), 8), :]
-            wn[:, pl.ds(pl.multiple_of(b * BLK, BLK), BLK)] = dot_t(rows, rbv[b])[:3]
-        return carry
-
-    lax.fori_loop(0, BLOCKS // 16, wall, 0)
+            wn[:, b * BLK : (b + 1) * BLK] = dot_t(local[b * 8 : b * 8 + 8, :], rbv[b])[:3]
+        points = pl.ds(i * 16 * BLK, 16 * BLK)
+        copies.append(pltpu.make_async_copy(wn.at[:, points], wn_out.at[:, points], sems.at[5 + i]))
+        copies[-1].start()
     for copy in copies:
         copy.wait()
 
@@ -511,9 +505,9 @@
             jax.ShapeDtypeStruct((3, POINTS), F32),
             jax.ShapeDtypeStruct((1, 1), F32),
         ),
-        in_specs=[vmem] * 5,
-        out_specs=(any_, any_, vmem, any_),
-        scratch_shapes=[pltpu.SemaphoreType.DMA((5,))],
+        in_specs=[vmem, vmem, vmem, any_, vmem],
+        out_specs=(any_,) * 4,
+        scratch_shapes=[pltpu.VMEM((3, POINTS), F32), pltpu.SemaphoreType.DMA((9,))],
         compiler_params=pltpu.CompilerParams(vmem_limit_bytes=8 << 20),
     )(*out)
     moved = jnp.transpose(moved.reshape(3, ROWS, 128), (1, 0, 2))

time: 54.5 us -> 48.7 us (0.89)
  Pallas kernels: 53.7 us -> 48 us
    pallas_call x1, Pallas kernels: 49.7 us -> 44.5 us  [per_device(): pl.pallas_call(kernel, name='coupling', out_shape=(pltpu.VMEM((3, POINTS,...]
    pallas_call x1, Pallas kernels: 4.03 us -> 3.42 us  [per_device(): pl.pallas_call(finish, name='wall', out_shape=(jax.ShapeDtypeStruct((3, P...]
where the time goes in v2:
time: 48.7 us; the launch traced here: 48.6 us
  Pallas kernels  48 us (99%)
  between operations  0.64 us (1%)
    pallas_call x1, Pallas kernels, per_device(): pl.pallas_call(kernel, name='coupling', out_shape=(pltpu.VMEM((3, POINTS,...  44.5 us
    pallas_call x1, Pallas kernels, per_device(): pl.pallas_call(finish, name='wall', out_shape=(jax.ShapeDtypeStruct((3, P...  3.42 us

profile of v2, /device:TPU:1, one launch (start us, length us, event | category | flops | bytes accessed | tf_op | source)
XLA Modules:
  0.0 48.6 jit_solution(14794883466678885832)
XLA Ops:
  0.6 44.5 %coupling.1 = (bf16[3,8192,128]{2,1,0:T(8,128)(2,1)S(1)}, f32[96,128]{1,0:T(8,128)S(1)}, bf16[512,128]{1,0:T(8,128)(2,1)S(1)}, f32[1,1]{1,0:T(1,128)}, bf16[64,128,128]{2,1,0:T(8,128)(2,1)S(1)}) custom-call(bf16[3,8192,128]{2,1,0:T(8,128)(2,1)} %flow.1, f32[3,8192]{1,0:T(4,128)} %wm.1, bf16[128,128]{1,0:T(8,128)(2,1)} %aop.1, f32[1,128]{1,0:T(1,128)} %bitcast.18, ...), custom_call_target="tpu_custom_call" | custom-call | tf_op jit(solution)/shard_map/coupling/pallas_call | solution.py:441
  45.2 3.4 %wall.1 = (bf16[3,8192,128]{2,1,0:T(8,128)(2,1)}, f32[96,128]{1,0:T(8,128)}, f32[3,8192]{1,0:T(4,128)}, f32[1,1]{1,0:T(1,128)}) custom-call(bf16[3,8192,128]{2,1,0:T(8,128)(2,1)S(1)} %get-tuple-element.13.nf, f32[96,128]{1,0:T(8,128)S(1)} %get-tuple-element.14.nd, bf16[512,128]{1,0:T(8,128)(2,1)S(1)} %get-tuple-element.15.local, ...), custom_call_target="tpu_custom_call" | custom-call | tf_op jit(solution)/shard_map/wall/pallas_call | solution.py:499

commit v3 on v2

--- a/solution.py
+++ b/solution.py
@@ -45,7 +45,7 @@
     nf, nd, local, norm, rbv,
     fbuf, wmv, av, wcv, wsv, ownv, rowv, dbuf, sbuf, vv, wv,
     mapped, oh, oht, lab, gsend, gin1, gsum1, gin2, out, arrived, pt, fext,
-    psend, pin, cbuf, rep, back, resid, wide32, tract,
+    psend, pin, cbuf, rep, back, resid, late, wide32, tract,
     lsem, ssem, rsem,
 ):
     f, s = lax.axis_index("fluid"), lax.axis_index("solid")
@@ -316,38 +316,47 @@
         taken(dbuf.at[:, pl.ds(0, 8), :], rsem.at[i])
     for i in (4, 5):
         taken(sbuf.at[pl.ds(0, 8), :], rsem.at[i])
-    for i in (9, 10):
-        taken(fext.at[:, pl.ds(0, 8), :], rsem.at[i])
 
     long = ROWS + 16
     at_row = iota((3, long, 128), 1) + me * ROWS - 8
     inside = (at_row >= 0) & (at_row < ND * ROWS)
     inverse = jnp.where(inside, 1.0 / (4.0 + sbuf[...])[None], 0.0)
-    loads = jnp.where(inside, fext[...], 0.0)
-    solved = jnp.where(inside, dbuf[...], 0.0)
-    start = solved[:, 8 : 8 + ROWS]
+    begin = jnp.where(inside, dbuf[...], 0.0)
     q = iota((3, long, 128), 2)
-    for _ in range(SWEEPS):
-        zero = jnp.zeros((3, 1, 128), F32)
-        up = jnp.concatenate([zero, solved[:, : long - 1]], axis=1)
-        down = jnp.concatenate([solved[:, 1:], zero], axis=1)
-        left = jnp.where(q == 0, 0.0, pltpu.roll(solved, 1, 2))
-        right = jnp.where(q == 127, 0.0, pltpu.roll(solved, 127, 2))
-        solved = (loads + ((up + down) + (left + right))) * inverse
-    solved = solved[:, 8 : 8 + ROWS]
-    residual = (solved - start).reshape(ENT, 128)
-    solved = solved.reshape(ENT, 128)
-
-    resid[...] = residual
-
-    def project(t, accs):
+
+    def sweep(loads):
+        solved = begin
+        for _ in range(SWEEPS):
+            zero = jnp.zeros((3, 1, 128), F32)
+            up = jnp.concatenate([zero, solved[:, : long - 1]], axis=1)
+            down = jnp.concatenate([solved[:, 1:], zero], axis=1)
+            left = jnp.where(q == 0, 0.0, pltpu.roll(solved, 1, 2))
+            right = jnp.where(q == 127, 0.0, pltpu.roll(solved, 127, 2))
+            solved = (loads + ((up + down) + (left + right))) * inverse
+        solved = solved[:, 8 : 8 + ROWS]
+        return solved.reshape(ENT, 128), (solved - begin[:, 8 : 8 + ROWS]).reshape(ENT, 128)
+
+    def project(rows, ref, accs):
         accs = list(accs)
-        for u in range(48):
-            i = t * 48 + u
-            accs[u % 4] = accs[u % 4] + history(i) * resid[pl.ds(i, 1), :]
-        return tuple(accs)
-
-    accs = lax.fori_loop(0, 2, project, (jnp.zeros((HIST, 128), F32),) * 4)
+        for n, r in enumerate(rows):
+            for c in range(3):
+                i = c * ROWS + r
+                u = (n * 3 + c) % 4
+                accs[u] = accs[u] + history(i) * ref[i : i + 1, :]
+        return accs
+
+    none = jnp.zeros((3, 8, 128), F32)
+    resid[...] = sweep(jnp.concatenate([none, force[:ENT].reshape(3, ROWS, 128), none], axis=1))[1]
+    accs = project(range(3, ROWS - 3), resid, [jnp.zeros((HIST, 128), F32)] * 4)
+
+
+    for i in (9, 10):
+        taken(fext.at[:, pl.ds(0, 8), :], rsem.at[i])
+
+    solved, residual = sweep(jnp.where(inside, fext[...], 0.0))
+    late[...] = residual
+    accs = project(range(3), late, accs)
+    accs = project(range(ROWS - 3, ROWS), late, accs)
     proj = (accs[0] + accs[1]) + (accs[2] + accs[3])
     square = jnp.sum((residual * residual).reshape(ENT // 8, 8, 128), axis=0)
     sums = jnp.concatenate([proj, square, jnp.zeros((128 - HIST - 8, 128), F32)], axis=0)
@@ -480,6 +489,7 @@
             pltpu.VMEM((NF, SLOTS, 128), BF16),
             pltpu.VMEM((NF, SLOTS, 128), BF16),
             pltpu.VMEM((ENT, 128), F32),
+            pltpu.VMEM((ENT, 128), F32),
             pltpu.VMEM((24, BLK + 2 * EDGE, 128), F32),
             pltpu.VMEM((BLOCKS, 16, 128), BF16),
             pltpu.SemaphoreType.DMA((11 + CHUNKS,)),

time: 48.7 us -> 48.3 us (level)
  Pallas kernels: 48 us -> 47.5 us
where the time goes in v3:
time: 48.3 us; the launch traced here: 48.1 us
  Pallas kernels  47.5 us (98%)
  between operations  0.64 us (1%)
    pallas_call x1, Pallas kernels, per_device(): pl.pallas_call(kernel, name='coupling', out_shape=(pltpu.VMEM((3, POINTS,...  44.1 us
    pallas_call x1, Pallas kernels, per_device(): pl.pallas_call(finish, name='wall', out_shape=(jax.ShapeDtypeStruct((3, P...  3.42 us

profile of v3, /device:TPU:1, one launch (start us, length us, event | category | flops | bytes accessed | tf_op | source)
XLA Modules:
  0.0 48.1 jit_solution(12000945301740421514)
XLA Ops:
  0.6 44.1 %coupling.1 = (bf16[3,8192,128]{2,1,0:T(8,128)(2,1)S(1)}, f32[96,128]{1,0:T(8,128)S(1)}, bf16[512,128]{1,0:T(8,128)(2,1)S(1)}, f32[1,1]{1,0:T(1,128)}, bf16[64,128,128]{2,1,0:T(8,128)(2,1)S(1)}) custom-call(bf16[3,8192,128]{2,1,0:T(8,128)(2,1)} %flow.1, f32[3,8192]{1,0:T(4,128)} %wm.1, bf16[128,128]{1,0:T(8,128)(2,1)} %aop.1, f32[1,128]{1,0:T(1,128)} %bitcast.18, ...), custom_call_target="tpu_custom_call" | custom-call | tf_op jit(solution)/shard_map/coupling/pallas_call | solution.py:450
  44.7 3.4 %wall.1 = (bf16[3,8192,128]{2,1,0:T(8,128)(2,1)}, f32[96,128]{1,0:T(8,128)}, f32[3,8192]{1,0:T(4,128)}, f32[1,1]{1,0:T(1,128)}) custom-call(bf16[3,8192,128]{2,1,0:T(8,128)(2,1)S(1)} %get-tuple-element.13.nf, f32[96,128]{1,0:T(8,128)S(1)} %get-tuple-element.14.nd, bf16[512,128]{1,0:T(8,128)(2,1)S(1)} %get-tuple-element.15.local, ...), custom_call_target="tpu_custom_call" | custom-call | tf_op jit(solution)/shard_map/wall/pallas_call | solution.py:509

commit v4 on v3

--- a/solution.py
+++ b/solution.py
@@ -368,12 +368,12 @@
     psend[...] = line
     pin[me] = line
 
-    def tell(d, carry):
-        other = lax.rem(me + d, ND)
+    def tell(k, carry):
+        other = lax.rem(me + ND + (1 - 2 * lax.rem(k, 2)) * (k // 2 + 1), ND)
         send(psend, pin.at[me], 11, (other // NS, lax.rem(other, NS)))
         return carry
 
-    lax.fori_loop(1, ND, tell, 0)
+    lax.fori_loop(0, ND - 1, tell, 0)
 
     taken(gin2.at[pl.ds(0, 15)], rsem.at[7])
     total = gin2[0]

time: 48.3 us -> 48.9 us (1.012)
  Pallas kernels: 47.5 us -> 48.1 us
    pallas_call x1, Pallas kernels: 44.1 us -> 44.7 us  [per_device(): pl.pallas_call(kernel, name='coupling', out_shape=(pltpu.VMEM((3, POINTS,...]
where the time goes in v4:
time: 48.9 us; the launch traced here: 48.7 us
  Pallas kernels  48.1 us (98%)
  between operations  0.64 us (1%)
    pallas_call x1, Pallas kernels, per_device(): pl.pallas_call(kernel, name='coupling', out_shape=(pltpu.VMEM((3, POINTS,...  44.7 us
    pallas_call x1, Pallas kernels, per_device(): pl.pallas_call(finish, name='wall', out_shape=(jax.ShapeDtypeStruct((3, P...  3.42 us

profile of v4, /device:TPU:1, one launch (start us, length us, event | category | flops | bytes accessed | tf_op | source)
XLA Modules:
  0.0 48.7 jit_solution(13216703826547957013)
XLA Ops:
  0.6 44.7 %coupling.1 = (bf16[3,8192,128]{2,1,0:T(8,128)(2,1)S(1)}, f32[96,128]{1,0:T(8,128)S(1)}, bf16[512,128]{1,0:T(8,128)(2,1)S(1)}, f32[1,1]{1,0:T(1,128)}, bf16[64,128,128]{2,1,0:T(8,128)(2,1)S(1)}) custom-call(bf16[3,8192,128]{2,1,0:T(8,128)(2,1)} %flow.1, f32[3,8192]{1,0:T(4,128)} %wm.1, bf16[128,128]{1,0:T(8,128)(2,1)} %aop.1, f32[1,128]{1,0:T(1,128)} %bitcast.18, ...), custom_call_target="tpu_custom_call" | custom-call | tf_op jit(solution)/shard_map/coupling/pallas_call | solution.py:450
  45.3 3.4 %wall.1 = (bf16[3,8192,128]{2,1,0:T(8,128)(2,1)}, f32[96,128]{1,0:T(8,128)}, f32[3,8192]{1,0:T(4,128)}, f32[1,1]{1,0:T(1,128)}) custom-call(bf16[3,8192,128]{2,1,0:T(8,128)(2,1)S(1)} %get-tuple-element.13.nf, f32[96,128]{1,0:T(8,128)S(1)} %get-tuple-element.14.nd, bf16[512,128]{1,0:T(8,128)(2,1)S(1)} %get-tuple-element.15.local, ...), custom_call_target="tpu_custom_call" | custom-call | tf_op jit(solution)/shard_map/wall/pallas_call | solution.py:509
